TPU v7x, 256 devices: a whole 4x4x8 slice. The times are simulated.
256 devices in a mesh: row: 16 (over z, core), col: 16 (over x, y).
Axes of the slice: x: 4, y: 4, z: 8, core: 2. Of those that a mesh axis runs over, the one named last changes fastest.
Arguments:
- rhs: float32 [16, 64, 128], P('col'), may hold values from -6 to 6
- diag_inv: float32 [16, 128, 128], P('col'), as said below
- panel: bfloat16 [16, 16, 128, 128], P('row', 'col'), may hold values from -0.09375 to 0.09375
- offdiag: bfloat16 [1024, 16, 128, 128], P('row', 'col'), may hold values from -0.015625 to 0.015625
- known: bfloat16 [512, 64, 128], P(('row', 'col')), may hold values from -6 to 6
- row_index: int32 [1024], P('row'), may hold values from 0 to 31
Outputs:
- solution: bfloat16 [16, 64, 128], P('col')
Inputs may be any that keep to these rules, and one draw needn't show every extreme that they name: Each block of diag_inv is lower triangular (the inverse of a lower triangular diagonal block).
All inputs are finite; a program needn't handle non-finite values.
Results may differ from a plain program's by a relative error of at most 0.015.
Values may be sent and summed in bfloat16 or wider, within the bound.
A program may use at most 64 MiB of HBM per device.

v0:
```python
import jax
import jax.numpy as jnp
from jax import lax
from jax.sharding import PartitionSpec as P

NB = 16


def spread(array, axis, root):
    mine = lax.axis_index(axis) == root
    return lax.psum(jnp.where(mine, array, jnp.zeros_like(array)), axis)


def finish_block(total, inverse, turn_block, root, solved):
    local = jnp.dot(
        total, inverse, precision=lax.Precision.HIGHEST, preferred_element_type=jnp.float32
    ).astype(jnp.bfloat16)
    block = spread(local, "col", root)
    solved = lax.dynamic_update_index_in_dim(solved, block, turn_block, 0)
    return (block, solved)


def body(rhs, diag_inv, panel, offdiag, known, row_index):
    rows_count = lax.axis_size("row")
    cols_count = lax.axis_size("col")
    row_id = lax.axis_index("row")
    col_id = lax.axis_index("col")
    col_slots = NB // cols_count
    known_row = lax.all_gather(known, "col", axis=0, tiled=True)
    picked = jnp.take(known_row, row_index, axis=0)
    off_part = jnp.einsum("pqi,pbia->bqa", picked, offdiag, preferred_element_type=jnp.float32)
    off_sum = lax.psum(off_part, "row")
    update = rhs - off_sum
    col_global = jnp.arange(col_slots) * cols_count + col_id
    accum = jnp.zeros(update.shape, jnp.float32)
    solved = jnp.zeros((NB,) + update.shape[1:], jnp.bfloat16)

    def step_reduced(turn, carry):
        sums, result = carry
        block_id = NB - 1 - turn
        slot = block_id // cols_count
        partial_value = lax.dynamic_index_in_dim(sums, slot, 0, keepdims=False)
        summed = lax.psum(partial_value.astype(jnp.bfloat16), "row").astype(jnp.float32)
        total = lax.dynamic_index_in_dim(update, slot, 0, keepdims=False) - summed
        inverse = lax.dynamic_index_in_dim(diag_inv, slot, 0, keepdims=False)
        block, result = finish_block(total, inverse, block_id, block_id % cols_count, result)
        tiles = lax.dynamic_index_in_dim(panel, block_id // rows_count, 0, keepdims=False)
        contrib = jnp.einsum("qi,bia->bqa", block, tiles, preferred_element_type=jnp.float32)
        keep = (col_global < block_id) & (block_id % rows_count == row_id)
        return (sums + jnp.where(keep[:, None, None], contrib, 0.0), result)

    accum, solved = lax.fori_loop(0, NB, step_reduced, (accum, solved))
    return jnp.take(solved, col_global, axis=0)


def solution(mesh):
    placed = (
        P("col", None, None),
        P("col", None, None),
        P("row", "col", None, None),
        P("row", "col", None, None),
        P(("row", "col"), None, None),
        P("row"),
    )
    return jax.shard_map(
        body, mesh=mesh, in_specs=placed, out_specs=P("col", None, None), check_vma=False
    )
```

profile of v0, /device:TPU:0, one launch (start us, length us, event | category | flops | bytes accessed | tf_op | source)
XLA Modules:
  0.0 1928.7 jit_solution(12652828160161664547)
XLA Ops:
  26.9 48.6 %psum.35 = f32[1,64,128]{2,1,0:T(8,128)S(1)} all-reduce(f32[1,64,128]{2,1,0:T(8,128)S(1)} %fusion.9), channel_id=1, replica_groups=mesh['row'=16,'col'=16] {'row'}, use_global_device_ids=true, to_apply=%region_0.1 | all-reduce | flops 8192 | bytes 65536 | tf_op jit(solution)/shard_map/psum | solution.py:32
  75.6 1852.5 %while.19 = (s32[]{:T(128)}, f32[1,64,128]{2,1,0:T(8,128)S(1)}, bf16[16,64,128]{2,1,0:T(8,128)(2,1)S(1)}, s32[1]{0:T(128)}, s32[]{:T(128)}, /*index=5*/f32[1,64,...) while((s32[]{:T(128)}, f32[1,64,128]{2,1,0:T(8,128)S(1)}, ...), condition=%wide.region_4.5_spmd.clone, body=%wide.region_1.0_spmd.clone.sunk | while | flops 14762007 | bytes 393562 | solution.py:52
  75.6 45.7 %psum.40 = bf16[64,128]{1,0:T(8,128)(2,1)S(1)} all-reduce(bf16[64,128]{1,0:T(8,128)(2,1)S(1)} %fusion.26), channel_id=1, replica_groups=mesh['row'=16,'col'=16] {'row'}, use_global_device_ids=true, to_apply=%region_2.2 | all-reduce | flops 8192 | bytes 32768 | tf_op jit(solution)/shard_map/while/body/eval_jaxpr/psum | solution.py:43
  121.5 72.1 %psum.41 = bf16[64,128]{1,0:T(8,128)(2,1)S(1)} all-reduce(bf16[64,128]{1,0:T(8,128)(2,1)S(1)} %fusion.27), channel_id=1, replica_groups=mesh['row'=16,'col'=16] {'col'}, use_global_device_ids=true, to_apply=%region_3.3 | all-reduce | flops 8192 | bytes 32768 | tf_op jit(solution)/shard_map/while/body/eval_jaxpr/psum | solution.py:11
  239.7 69.6 %psum.41 = bf16[64,128]{1,0:T(8,128)(2,1)S(1)} all-reduce(bf16[64,128]{1,0:T(8,128)(2,1)S(1)} %fusion.27), channel_id=1, replica_groups=mesh['row'=16,'col'=16] {'col'}, use_global_device_ids=true, to_apply=%region_3.3 | all-reduce | flops 8192 | bytes 32768 | tf_op jit(solution)/shard_map/while/body/eval_jaxpr/psum | solution.py:11
  309.4 45.7 %psum.40 = bf16[64,128]{1,0:T(8,128)(2,1)S(1)} all-reduce(bf16[64,128]{1,0:T(8,128)(2,1)S(1)} %fusion.26), channel_id=1, replica_groups=mesh['row'=16,'col'=16] {'row'}, use_global_device_ids=true, to_apply=%region_2.2 | all-reduce | flops 8192 | bytes 32768 | tf_op jit(solution)/shard_map/while/body/eval_jaxpr/psum | solution.py:43
  355.3 69.6 %psum.41 = bf16[64,128]{1,0:T(8,128)(2,1)S(1)} all-reduce(bf16[64,128]{1,0:T(8,128)(2,1)S(1)} %fusion.27), channel_id=1, replica_groups=mesh['row'=16,'col'=16] {'col'}, use_global_device_ids=true, to_apply=%region_3.3 | all-reduce | flops 8192 | bytes 32768 | tf_op jit(solution)/shard_map/while/body/eval_jaxpr/psum | solution.py:11
  425.0 45.7 %psum.40 = bf16[64,128]{1,0:T(8,128)(2,1)S(1)} all-reduce(bf16[64,128]{1,0:T(8,128)(2,1)S(1)} %fusion.26), channel_id=1, replica_groups=mesh['row'=16,'col'=16] {'row'}, use_global_device_ids=true, to_apply=%region_2.2 | all-reduce | flops 8192 | bytes 32768 | tf_op jit(solution)/shard_map/while/body/eval_jaxpr/psum | solution.py:43
  470.9 69.6 %psum.41 = bf16[64,128]{1,0:T(8,128)(2,1)S(1)} all-reduce(bf16[64,128]{1,0:T(8,128)(2,1)S(1)} %fusion.27), channel_id=1, replica_groups=mesh['row'=16,'col'=16] {'col'}, use_global_device_ids=true, to_apply=%region_3.3 | all-reduce | flops 8192 | bytes 32768 | tf_op jit(solution)/shard_map/while/body/eval_jaxpr/psum | solution.py:11
  586.6 69.6 %psum.41 = bf16[64,128]{1,0:T(8,128)(2,1)S(1)} all-reduce(bf16[64,128]{1,0:T(8,128)(2,1)S(1)} %fusion.27), channel_id=1, replica_groups=mesh['row'=16,'col'=16] {'col'}, use_global_device_ids=true, to_apply=%region_3.3 | all-reduce | flops 8192 | bytes 32768 | tf_op jit(solution)/shard_map/while/body/eval_jaxpr/psum | solution.py:11
  702.2 69.6 %psum.41 = bf16[64,128]{1,0:T(8,128)(2,1)S(1)} all-reduce(bf16[64,128]{1,0:T(8,128)(2,1)S(1)} %fusion.27), channel_id=1, replica_groups=mesh['row'=16,'col'=16] {'col'}, use_global_device_ids=true, to_apply=%region_3.3 | all-reduce | flops 8192 | bytes 32768 | tf_op jit(solution)/shard_map/while/body/eval_jaxpr/psum | solution.py:11
  771.9 45.7 %psum.40 = bf16[64,128]{1,0:T(8,128)(2,1)S(1)} all-reduce(bf16[64,128]{1,0:T(8,128)(2,1)S(1)} %fusion.26), channel_id=1, replica_groups=mesh['row'=16,'col'=16] {'row'}, use_global_device_ids=true, to_apply=%region_2.2 | all-reduce | flops 8192 | bytes 32768 | tf_op jit(solution)/shard_map/while/body/eval_jaxpr/psum | solution.py:43
  817.8 69.6 %psum.41 = bf16[64,128]{1,0:T(8,128)(2,1)S(1)} all-reduce(bf16[64,128]{1,0:T(8,128)(2,1)S(1)} %fusion.27), channel_id=1, replica_groups=mesh['row'=16,'col'=16] {'col'}, use_global_device_ids=true, to_apply=%region_3.3 | all-reduce | flops 8192 | bytes 32768 | tf_op jit(solution)/shard_map/while/body/eval_jaxpr/psum | solution.py:11
  887.5 45.7 %psum.40 = bf16[64,128]{1,0:T(8,128)(2,1)S(1)} all-reduce(bf16[64,128]{1,0:T(8,128)(2,1)S(1)} %fusion.26), channel_id=1, replica_groups=mesh['row'=16,'col'=16] {'row'}, use_global_device_ids=true, to_apply=%region_2.2 | all-reduce | flops 8192 | bytes 32768 | tf_op jit(solution)/shard_map/while/body/eval_jaxpr/psum | solution.py:43
  933.4 69.6 %psum.41 = bf16[64,128]{1,0:T(8,128)(2,1)S(1)} all-reduce(bf16[64,128]{1,0:T(8,128)(2,1)S(1)} %fusion.27), channel_id=1, replica_groups=mesh['row'=16,'col'=16] {'col'}, use_global_device_ids=true, to_apply=%region_3.3 | all-reduce | flops 8192 | bytes 32768 | tf_op jit(solution)/shard_map/while/body/eval_jaxpr/psum | solution.py:11
  1049.0 69.6 %psum.41 = bf16[64,128]{1,0:T(8,128)(2,1)S(1)} all-reduce(bf16[64,128]{1,0:T(8,128)(2,1)S(1)} %fusion.27), channel_id=1, replica_groups=mesh['row'=16,'col'=16] {'col'}, use_global_device_ids=true, to_apply=%region_3.3 | all-reduce | flops 8192 | bytes 32768 | tf_op jit(solution)/shard_map/while/body/eval_jaxpr/psum | solution.py:11
  1118.7 45.7 %psum.40 = bf16[64,128]{1,0:T(8,128)(2,1)S(1)} all-reduce(bf16[64,128]{1,0:T(8,128)(2,1)S(1)} %fusion.26), channel_id=1, replica_groups=mesh['row'=16,'col'=16] {'row'}, use_global_device_ids=true, to_apply=%region_2.2 | all-reduce | flops 8192 | bytes 32768 | tf_op jit(solution)/shard_map/while/body/eval_jaxpr/psum | solution.py:43
  1164.7 69.6 %psum.41 = bf16[64,128]{1,0:T(8,128)(2,1)S(1)} all-reduce(bf16[64,128]{1,0:T(8,128)(2,1)S(1)} %fusion.27), channel_id=1, replica_groups=mesh['row'=16,'col'=16] {'col'}, use_global_device_ids=true, to_apply=%region_3.3 | all-reduce | flops 8192 | bytes 32768 | tf_op jit(solution)/shard_map/while/body/eval_jaxpr/psum | solution.py:11
  1280.3 69.6 %psum.41 = bf16[64,128]{1,0:T(8,128)(2,1)S(1)} all-reduce(bf16[64,128]{1,0:T(8,128)(2,1)S(1)} %fusion.27), channel_id=1, replica_groups=mesh['row'=16,'col'=16] {'col'}, use_global_device_ids=true, to_apply=%region_3.3 | all-reduce | flops 8192 | bytes 32768 | tf_op jit(solution)/shard_map/while/body/eval_jaxpr/psum | solution.py:11
  1395.9 69.6 %psum.41 = bf16[64,128]{1,0:T(8,128)(2,1)S(1)} all-reduce(bf16[64,128]{1,0:T(8,128)(2,1)S(1)} %fusion.27), channel_id=1, replica_groups=mesh['row'=16,'col'=16] {'col'}, use_global_device_ids=true, to_apply=%region_3.3 | all-reduce | flops 8192 | bytes 32768 | tf_op jit(solution)/shard_map/while/body/eval_jaxpr/psum | solution.py:11
  1511.5 69.6 %psum.41 = bf16[64,128]{1,0:T(8,128)(2,1)S(1)} all-reduce(bf16[64,128]{1,0:T(8,128)(2,1)S(1)} %fusion.27), channel_id=1, replica_groups=mesh['row'=16,'col'=16] {'col'}, use_global_device_ids=true, to_apply=%region_3.3 | all-reduce | flops 8192 | bytes 32768 | tf_op jit(solution)/shard_map/while/body/eval_jaxpr/psum | solution.py:11
  1627.1 69.6 %psum.41 = bf16[64,128]{1,0:T(8,128)(2,1)S(1)} all-reduce(bf16[64,128]{1,0:T(8,128)(2,1)S(1)} %fusion.27), channel_id=1, replica_groups=mesh['row'=16,'col'=16] {'col'}, use_global_device_ids=true, to_apply=%region_3.3 | all-reduce | flops 8192 | bytes 32768 | tf_op jit(solution)/shard_map/while/body/eval_jaxpr/psum | solution.py:11
  1742.7 69.6 %psum.41 = bf16[64,128]{1,0:T(8,128)(2,1)S(1)} all-reduce(bf16[64,128]{1,0:T(8,128)(2,1)S(1)} %fusion.27), channel_id=1, replica_groups=mesh['row'=16,'col'=16] {'col'}, use_global_device_ids=true, to_apply=%region_3.3 | all-reduce | flops 8192 | bytes 32768 | tf_op jit(solution)/shard_map/while/body/eval_jaxpr/psum | solution.py:11
  1858.4 69.6 %psum.41 = bf16[64,128]{1,0:T(8,128)(2,1)S(1)} all-reduce(bf16[64,128]{1,0:T(8,128)(2,1)S(1)} %fusion.27), channel_id=1, replica_groups=mesh['row'=16,'col'=16] {'col'}, use_global_device_ids=true, to_apply=%region_3.3 | all-reduce | flops 8192 | bytes 32768 | tf_op jit(solution)/shard_map/while/body/eval_jaxpr/psum | solution.py:11
  (94 shorter events, 490.0 us)
Async XLA Ops:
  0.0 25.0 %copy-start = (bf16[64,1,128,128]{3,2,1,0:T(8,128)(2,1)S(1)}, bf16[64,1,128,128]{3,2,1,0:T(8,128)(2,1)}, u32[]{:S(2)}) copy-start(bf16[64,1,128,128]{3,2,1,0:T(8,128)(2,1)} %param.11) | copy-start | bytes 6291460
  0.0 25.0 %copy-start.4 = (s32[64]{0:T(128)S(1)}, s32[64]{0:T(128)}, u32[]{:S(2)}) copy-start(s32[64]{0:T(128)} %param.13) | copy-start | bytes 772
  25.0 50.5 %copy-start.3 = (f32[1,64,128]{2,1,0:T(8,128)S(1)}, f32[1,64,128]{2,1,0:T(8,128)}, u32[]{:S(2)}) copy-start(f32[1,64,128]{2,1,0:T(8,128)} %param.8) | copy-start | bytes 98308
  25.0 50.6 %copy-start.1 = (f32[1,128,128]{2,1,0:T(8,128)S(1)}, f32[1,128,128]{2,1,0:T(8,128)}, u32[]{:S(2)}) copy-start(f32[1,128,128]{2,1,0:T(8,128)} %param.9) | copy-start | bytes 196612
  25.0 50.6 %copy-start.2 = (bf16[1,1,128,128]{3,2,1,0:T(8,128)(2,1)S(1)}, bf16[1,1,128,128]{3,2,1,0:T(8,128)(2,1)}, u32[]{:S(2)}) copy-start(bf16[1,1,128,128]{3,2,1,0:T(8,128)(2,1)} %param.10) | copy-start | bytes 98308
where the time goes:
time: 1930 us
  blocking collectives  1920 us (99%)
    psum x16, blocking collectives, spread(): return lax.psum(jnp.where(mine, array, jnp.zeros_like(array)), axis)  1120 us
    psum x16, blocking collectives, step_reduced(): lax.psum(partial_value.astype(jnp.bfloat16), 'row').astype(jnp.float32)  732 us
    psum x1, blocking collectives, body(): off_sum = lax.psum(off_part, 'row')  48.6 us

commit v1 on v0

--- a/solution.py
+++ b/solution.py
@@ -8,7 +8,7 @@
 
 def spread(array, axis, root):
     mine = lax.axis_index(axis) == root
-    return lax.psum(jnp.where(mine, array, jnp.zeros_like(array)), axis)
+    return jnp.sum(lax.all_gather(jnp.where(mine, array, jnp.zeros_like(array)), axis), axis=0)
 
 
 def finish_block(total, inverse, turn_block, root, solved):

time: 1930 us -> 1170 us (0.61)
  blocking collectives: 1920 us -> 1160 us
    psum x16 -> x0, blocking collectives: 1120 us -> none  [spread(): return lax.psum(jnp.where(mine, array, jnp.zeros_like(array)), axis)]
    all_gather x0 -> x16, blocking collectives: none -> 357 us  [spread(): lax.all_gather(jnp.where(mine, array, jnp.zeros_like(array)), axis)]
where the time goes in v1:
time: 1170 us
  blocking collectives  1160 us (99%)
    psum x16, blocking collectives, step_reduced(): lax.psum(partial_value.astype(jnp.bfloat16), 'row').astype(jnp.float32)  732 us
    all_gather x16, blocking collectives, spread(): lax.all_gather(jnp.where(mine, array, jnp.zeros_like(array)), axis)  357 us
    psum x1, blocking collectives, body(): off_sum = lax.psum(off_part, 'row')  48.6 us

profile of v1, /device:TPU:0, one launch (start us, length us, event | category | flops | bytes accessed | tf_op | source)
XLA Modules:
  0.0 1171.5 jit_solution(3904346044898436378)
XLA Ops:
  26.9 48.6 %psum.21 = f32[1,64,128]{2,1,0:T(8,128)S(1)} all-reduce(f32[1,64,128]{2,1,0:T(8,128)S(1)} %fusion.9), channel_id=1, replica_groups=mesh['row'=16,'col'=16] {'row'}, use_global_device_ids=true, to_apply=%region_0.1 | all-reduce | flops 8192 | bytes 65536 | tf_op jit(solution)/shard_map/psum | solution.py:32
  75.6 1095.3 %while.19 = (s32[]{:T(128)}, f32[1,64,128]{2,1,0:T(8,128)S(1)}, bf16[16,64,128]{2,1,0:T(8,128)(2,1)S(1)}, s32[1]{0:T(128)}, s32[]{:T(128)}, /*index=5*/f32[1,64,...) while((s32[]{:T(128)}, f32[1,64,128]{2,1,0:T(8,128)S(1)}, ...), condition=%wide.region_4.5_spmd.clone, body=%wide.region_1.0_spmd.clone.sunk | while | flops 14876695 | bytes 917860 | solution.py:52
  75.6 45.7 %psum.24 = bf16[64,128]{1,0:T(8,128)(2,1)S(1)} all-reduce(bf16[64,128]{1,0:T(8,128)(2,1)S(1)} %fusion.26), channel_id=1, replica_groups=mesh['row'=16,'col'=16] {'row'}, use_global_device_ids=true, to_apply=%region_2.2 | all-reduce | flops 8192 | bytes 32768 | tf_op jit(solution)/shard_map/while/body/eval_jaxpr/psum | solution.py:43
  121.5 23.1 %all-gather.3 = bf16[1024,128]{1,0:T(8,128)(2,1)S(1)} all-gather(bf16[64,128]{1,0:T(8,128)(2,1)S(1)} %fusion.27), channel_id=2, replica_groups=mesh['row'=16,'col'=16] {'col'}, dimensions={0}, use_global_device_ids=true | all-gather | bytes 278528 | tf_op jit(solution)/shard_map/while/body/eval_jaxpr/all_gather | solution.py:11
  144.9 45.7 %psum.24 = bf16[64,128]{1,0:T(8,128)(2,1)S(1)} all-reduce(bf16[64,128]{1,0:T(8,128)(2,1)S(1)} %fusion.26), channel_id=1, replica_groups=mesh['row'=16,'col'=16] {'row'}, use_global_device_ids=true, to_apply=%region_2.2 | all-reduce | flops 8192 | bytes 32768 | tf_op jit(solution)/shard_map/while/body/eval_jaxpr/psum | solution.py:43
  212.5 45.7 %psum.24 = bf16[64,128]{1,0:T(8,128)(2,1)S(1)} all-reduce(bf16[64,128]{1,0:T(8,128)(2,1)S(1)} %fusion.26), channel_id=1, replica_groups=mesh['row'=16,'col'=16] {'row'}, use_global_device_ids=true, to_apply=%region_2.2 | all-reduce | flops 8192 | bytes 32768 | tf_op jit(solution)/shard_map/while/body/eval_jaxpr/psum | solution.py:43
  258.5 23.1 %all-gather.3 = bf16[1024,128]{1,0:T(8,128)(2,1)S(1)} all-gather(bf16[64,128]{1,0:T(8,128)(2,1)S(1)} %fusion.27), channel_id=2, replica_groups=mesh['row'=16,'col'=16] {'col'}, dimensions={0}, use_global_device_ids=true | all-gather | bytes 278528 | tf_op jit(solution)/shard_map/while/body/eval_jaxpr/all_gather | solution.py:11
  281.8 45.7 %psum.24 = bf16[64,128]{1,0:T(8,128)(2,1)S(1)} all-reduce(bf16[64,128]{1,0:T(8,128)(2,1)S(1)} %fusion.26), channel_id=1, replica_groups=mesh['row'=16,'col'=16] {'row'}, use_global_device_ids=true, to_apply=%region_2.2 | all-reduce | flops 8192 | bytes 32768 | tf_op jit(solution)/shard_map/while/body/eval_jaxpr/psum | solution.py:43
  349.5 45.7 %psum.24 = bf16[64,128]{1,0:T(8,128)(2,1)S(1)} all-reduce(bf16[64,128]{1,0:T(8,128)(2,1)S(1)} %fusion.26), channel_id=1, replica_groups=mesh['row'=16,'col'=16] {'row'}, use_global_device_ids=true, to_apply=%region_2.2 | all-reduce | flops 8192 | bytes 32768 | tf_op jit(solution)/shard_map/while/body/eval_jaxpr/psum | solution.py:43
  418.7 45.7 %psum.24 = bf16[64,128]{1,0:T(8,128)(2,1)S(1)} all-reduce(bf16[64,128]{1,0:T(8,128)(2,1)S(1)} %fusion.26), channel_id=1, replica_groups=mesh['row'=16,'col'=16] {'row'}, use_global_device_ids=true, to_apply=%region_2.2 | all-reduce | flops 8192 | bytes 32768 | tf_op jit(solution)/shard_map/while/body/eval_jaxpr/psum | solution.py:43
  486.4 45.7 %psum.24 = bf16[64,128]{1,0:T(8,128)(2,1)S(1)} all-reduce(bf16[64,128]{1,0:T(8,128)(2,1)S(1)} %fusion.26), channel_id=1, replica_groups=mesh['row'=16,'col'=16] {'row'}, use_global_device_ids=true, to_apply=%region_2.2 | all-reduce | flops 8192 | bytes 32768 | tf_op jit(solution)/shard_map/while/body/eval_jaxpr/psum | solution.py:43
  555.6 45.7 %psum.24 = bf16[64,128]{1,0:T(8,128)(2,1)S(1)} all-reduce(bf16[64,128]{1,0:T(8,128)(2,1)S(1)} %fusion.26), channel_id=1, replica_groups=mesh['row'=16,'col'=16] {'row'}, use_global_device_ids=true, to_apply=%region_2.2 | all-reduce | flops 8192 | bytes 32768 | tf_op jit(solution)/shard_map/while/body/eval_jaxpr/psum | solution.py:43
  623.3 45.7 %psum.24 = bf16[64,128]{1,0:T(8,128)(2,1)S(1)} all-reduce(bf16[64,128]{1,0:T(8,128)(2,1)S(1)} %fusion.26), channel_id=1, replica_groups=mesh['row'=16,'col'=16] {'row'}, use_global_device_ids=true, to_apply=%region_2.2 | all-reduce | flops 8192 | bytes 32768 | tf_op jit(solution)/shard_map/while/body/eval_jaxpr/psum | solution.py:43
  669.2 23.1 %all-gather.3 = bf16[1024,128]{1,0:T(8,128)(2,1)S(1)} all-gather(bf16[64,128]{1,0:T(8,128)(2,1)S(1)} %fusion.27), channel_id=2, replica_groups=mesh['row'=16,'col'=16] {'col'}, dimensions={0}, use_global_device_ids=true | all-gather | bytes 278528 | tf_op jit(solution)/shard_map/while/body/eval_jaxpr/all_gather | solution.py:11
  692.5 45.7 %psum.24 = bf16[64,128]{1,0:T(8,128)(2,1)S(1)} all-reduce(bf16[64,128]{1,0:T(8,128)(2,1)S(1)} %fusion.26), channel_id=1, replica_groups=mesh['row'=16,'col'=16] {'row'}, use_global_device_ids=true, to_apply=%region_2.2 | all-reduce | flops 8192 | bytes 32768 | tf_op jit(solution)/shard_map/while/body/eval_jaxpr/psum | solution.py:43
  760.2 45.7 %psum.24 = bf16[64,128]{1,0:T(8,128)(2,1)S(1)} all-reduce(bf16[64,128]{1,0:T(8,128)(2,1)S(1)} %fusion.26), channel_id=1, replica_groups=mesh['row'=16,'col'=16] {'row'}, use_global_device_ids=true, to_apply=%region_2.2 | all-reduce | flops 8192 | bytes 32768 | tf_op jit(solution)/shard_map/while/body/eval_jaxpr/psum | solution.py:43
  806.1 23.1 %all-gather.3 = bf16[1024,128]{1,0:T(8,128)(2,1)S(1)} all-gather(bf16[64,128]{1,0:T(8,128)(2,1)S(1)} %fusion.27), channel_id=2, replica_groups=mesh['row'=16,'col'=16] {'col'}, dimensions={0}, use_global_device_ids=true | all-gather | bytes 278528 | tf_op jit(solution)/shard_map/while/body/eval_jaxpr/all_gather | solution.py:11
  829.4 45.7 %psum.24 = bf16[64,128]{1,0:T(8,128)(2,1)S(1)} all-reduce(bf16[64,128]{1,0:T(8,128)(2,1)S(1)} %fusion.26), channel_id=1, replica_groups=mesh['row'=16,'col'=16] {'row'}, use_global_device_ids=true, to_apply=%region_2.2 | all-reduce | flops 8192 | bytes 32768 | tf_op jit(solution)/shard_map/while/body/eval_jaxpr/psum | solution.py:43
  897.1 45.7 %psum.24 = bf16[64,128]{1,0:T(8,128)(2,1)S(1)} all-reduce(bf16[64,128]{1,0:T(8,128)(2,1)S(1)} %fusion.26), channel_id=1, replica_groups=mesh['row'=16,'col'=16] {'row'}, use_global_device_ids=true, to_apply=%region_2.2 | all-reduce | flops 8192 | bytes 32768 | tf_op jit(solution)/shard_map/while/body/eval_jaxpr/psum | solution.py:43
  943.0 23.1 %all-gather.3 = bf16[1024,128]{1,0:T(8,128)(2,1)S(1)} all-gather(bf16[64,128]{1,0:T(8,128)(2,1)S(1)} %fusion.27), channel_id=2, replica_groups=mesh['row'=16,'col'=16] {'col'}, dimensions={0}, use_global_device_ids=true | all-gather | bytes 278528 | tf_op jit(solution)/shard_map/while/body/eval_jaxpr/all_gather | solution.py:11
  966.3 45.7 %psum.24 = bf16[64,128]{1,0:T(8,128)(2,1)S(1)} all-reduce(bf16[64,128]{1,0:T(8,128)(2,1)S(1)} %fusion.26), channel_id=1, replica_groups=mesh['row'=16,'col'=16] {'row'}, use_global_device_ids=true, to_apply=%region_2.2 | all-reduce | flops 8192 | bytes 32768 | tf_op jit(solution)/shard_map/while/body/eval_jaxpr/psum | solution.py:43
  1034.0 45.7 %psum.24 = bf16[64,128]{1,0:T(8,128)(2,1)S(1)} all-reduce(bf16[64,128]{1,0:T(8,128)(2,1)S(1)} %fusion.26), channel_id=1, replica_groups=mesh['row'=16,'col'=16] {'row'}, use_global_device_ids=true, to_apply=%region_2.2 | all-reduce | flops 8192 | bytes 32768 | tf_op jit(solution)/shard_map/while/body/eval_jaxpr/psum | solution.py:43
  1079.9 23.1 %all-gather.3 = bf16[1024,128]{1,0:T(8,128)(2,1)S(1)} all-gather(bf16[64,128]{1,0:T(8,128)(2,1)S(1)} %fusion.27), channel_id=2, replica_groups=mesh['row'=16,'col'=16] {'col'}, dimensions={0}, use_global_device_ids=true | all-gather | bytes 278528 | tf_op jit(solution)/shard_map/while/body/eval_jaxpr/all_gather | solution.py:11
  1103.3 45.7 %psum.24 = bf16[64,128]{1,0:T(8,128)(2,1)S(1)} all-reduce(bf16[64,128]{1,0:T(8,128)(2,1)S(1)} %fusion.26), channel_id=1, replica_groups=mesh['row'=16,'col'=16] {'row'}, use_global_device_ids=true, to_apply=%region_2.2 | all-reduce | flops 8192 | bytes 32768 | tf_op jit(solution)/shard_map/while/body/eval_jaxpr/psum | solution.py:43
  (110 shorter events, 252.0 us)
Async XLA Ops:
  0.0 25.0 %copy-start = (bf16[64,1,128,128]{3,2,1,0:T(8,128)(2,1)S(1)}, bf16[64,1,128,128]{3,2,1,0:T(8,128)(2,1)}, u32[]{:S(2)}) copy-start(bf16[64,1,128,128]{3,2,1,0:T(8,128)(2,1)} %param.11) | copy-start | bytes 6291460
  0.0 25.0 %copy-start.4 = (s32[64]{0:T(128)S(1)}, s32[64]{0:T(128)}, u32[]{:S(2)}) copy-start(s32[64]{0:T(128)} %param.13) | copy-start | bytes 772
  25.0 50.5 %copy-start.3 = (f32[1,64,128]{2,1,0:T(8,128)S(1)}, f32[1,64,128]{2,1,0:T(8,128)}, u32[]{:S(2)}) copy-start(f32[1,64,128]{2,1,0:T(8,128)} %param.8) | copy-start | bytes 98308
  25.0 50.6 %copy-start.1 = (f32[1,128,128]{2,1,0:T(8,128)S(1)}, f32[1,128,128]{2,1,0:T(8,128)}, u32[]{:S(2)}) copy-start(f32[1,128,128]{2,1,0:T(8,128)} %param.9) | copy-start | bytes 196612
  25.0 50.6 %copy-start.2 = (bf16[1,1,128,128]{3,2,1,0:T(8,128)(2,1)S(1)}, bf16[1,1,128,128]{3,2,1,0:T(8,128)(2,1)}, u32[]{:S(2)}) copy-start(bf16[1,1,128,128]{3,2,1,0:T(8,128)(2,1)} %param.10) | copy-start | bytes 98308
